TPU v7x, 32 devices: a whole 2x2x4 slice. The times are simulated.
32 devices in a mesh: dp: 8 (over y, x, core), tensor: 4 (over z).
Axes of the slice: x: 2, y: 2, z: 4, core: 2. Of those that a mesh axis runs over, the one named last changes fastest.
Arguments:
- block_in: float32 [4096, 1024], P(('dp', 'tensor')), may hold values from -6 to 6
- cotangent: float32 [4096, 1024], P(('dp', 'tensor')), may hold values from -6 to 6
- routes: int32 [4096, 8], P('dp'), may hold values from 0 to 15, all different within a row; in each aligned block of 512 rows (0 to 511, 512 to 1023, ...) at most 288 rows name the same one
- gate_weights: float32 [4096, 8], P('dp'), may hold values from 0.02 to 0.3
- norm_gains: float32 [2, 1024], P(None, 'dp'), may hold values from 0.5 to 1.5
- attention_weight: float32 [4, 1024, 512], P(None, 'dp', 'tensor'), may hold values from -0.1875 to 0.1875
- output_weight: float32 [2, 1024, 512], P(None, 'dp', 'tensor'), may hold values from -0.75 to 0.75
- w_gate_up: float32 [16, 2, 1024, 512], P(None, None, 'dp', 'tensor'), may hold values from -0.1875 to 0.1875
- w_down: float32 [16, 1024, 512], P(None, 'dp', 'tensor'), may hold values from -0.75 to 0.75
- m_gains: float32 [2, 1024], P(None, 'dp'), may hold values from -128 to 128
- v_gains: float32 [2, 1024], P(None, 'dp'), may hold values from 100 to 10000
- attention_first_moment: float32 [4, 1024, 512], P(None, 'dp', 'tensor'), may hold values from -12 to 12
- attention_second_moment: float32 [4, 1024, 512], P(None, 'dp', 'tensor'), may hold values from 1 to 100
- output_first_moment: float32 [2, 1024, 512], P(None, 'dp', 'tensor'), may hold values from -16 to 16
- output_second_moment: float32 [2, 1024, 512], P(None, 'dp', 'tensor'), may hold values from 1 to 100
- m_gate_up: float32 [16, 2, 1024, 512], P(None, None, 'dp', 'tensor'), may hold values from -32 to 32
- v_gate_up: float32 [16, 2, 1024, 512], P(None, None, 'dp', 'tensor'), may hold values from 10 to 1000
- m_down: float32 [16, 1024, 512], P(None, 'dp', 'tensor'), may hold values from -12 to 12
- v_down: float32 [16, 1024, 512], P(None, 'dp', 'tensor'), may hold values from 1 to 100
Outputs:
- block_out: float32 [4096, 1024], P(('dp', 'tensor'))
- input_grad: float32 [4096, 1024], P(('dp', 'tensor'))
- grad_gains: float32 [2, 1024], P(None, 'dp')
- grad_attn: float32 [4, 1024, 512], P(None, 'dp', 'tensor')
- grad_out: float32 [2, 1024, 512], P(None, 'dp', 'tensor')
- grad_gate_up: float32 [16, 2, 1024, 512], P(None, None, 'dp', 'tensor')
- grad_down: float32 [16, 1024, 512], P(None, 'dp', 'tensor')
- new_gains: float32 [2, 1024], P(None, 'dp')
- new_attn: float32 [4, 1024, 512], P(None, 'dp', 'tensor')
- new_out: float32 [2, 1024, 512], P(None, 'dp', 'tensor')
- new_gate_up: float32 [16, 2, 1024, 512], P(None, None, 'dp', 'tensor')
- new_down: float32 [16, 1024, 512], P(None, 'dp', 'tensor')
- new_m_gains: float32 [2, 1024], P(None, 'dp')
- new_v_gains: float32 [2, 1024], P(None, 'dp')
- new_m_attn: float32 [4, 1024, 512], P(None, 'dp', 'tensor')
- new_v_attn: float32 [4, 1024, 512], P(None, 'dp', 'tensor')
- new_m_out: float32 [2, 1024, 512], P(None, 'dp', 'tensor')
- new_v_out: float32 [2, 1024, 512], P(None, 'dp', 'tensor')
- new_m_gate_up: float32 [16, 2, 1024, 512], P(None, None, 'dp', 'tensor')
- new_v_gate_up: float32 [16, 2, 1024, 512], P(None, None, 'dp', 'tensor')
- new_m_down: float32 [16, 1024, 512], P(None, 'dp', 'tensor')
- new_v_down: float32 [16, 1024, 512], P(None, 'dp', 'tensor')
Inputs may be any that keep to these rules, and one draw needn't show every extreme that they name: `routes`: each row names 8 different experts. Within each aligned block of 512 rows no expert is named by more than 288 rows, and in some block one expert is named by exactly 288 rows.
All inputs are finite; a program needn't handle non-finite values.
Results may differ from a plain program's by a relative error of at most 0.015.
The roundings to bfloat16 on the way count: a program that leaves them out, or rounds other values in their place, can miss the bound.
Values may be sent and summed in bfloat16 or wider, within the bound.
A program may use at most 192 MiB of HBM per device.

v0:
```python
import jax
import jax.numpy as jnp
from jax import lax
from jax.sharding import PartitionSpec as P

HEAD_SIZE = 64
E = 16
SEQ = 512
STEP = 3
CAP = 288
norm_eps = 1e-05
beta_one = 0.9
beta_two = 0.95
adam_eps = 1e-08
rate_matrix = 0.02
rate_gain = 0.2
decay_matrix = 0.1
rope_base = 10000.0


def rope_tables(length, width):
    half_width = width // 2
    frequency = rope_base ** (-(2.0 * jnp.arange(half_width, dtype=jnp.float32)) / width)
    angles = jnp.arange(length, dtype=jnp.float32)[:, None] * frequency[None, :]
    return (jnp.cos(angles)[:, None, :], jnp.sin(angles)[:, None, :])


def rotate(vectors, cos_table, sine_table):
    half_width = vectors.shape[-1] // 2
    lower_half = vectors[..., :half_width]
    upper_half = vectors[..., half_width:]
    return jnp.concatenate(
        [
            lower_half * cos_table - upper_half * sine_table,
            upper_half * cos_table + lower_half * sine_table,
        ],
        axis=-1,
    )


def unrotate(vectors, cos_table, sine_table):
    half_width = vectors.shape[-1] // 2
    lower_half = vectors[..., :half_width]
    upper_half = vectors[..., half_width:]
    return jnp.concatenate(
        [
            lower_half * cos_table + upper_half * sine_table,
            upper_half * cos_table - lower_half * sine_table,
        ],
        axis=-1,
    )


def causal_scores(queries, keys_rot):
    scale = queries.shape[-1] ** (-0.5)
    scores = (
        jnp.einsum("jqgh,kgh->jgqk", queries, keys_rot, preferred_element_type=jnp.float32) * scale
    )
    length = scores.shape[-1]
    allowed = lax.broadcasted_iota(jnp.int32, (length, length), 0) >= lax.broadcasted_iota(
        jnp.int32, (length, length), 1
    )
    return jnp.where(allowed, scores, -jnp.inf)


def attend(items):
    queries, keys_rot, values = items
    scores = causal_scores(queries, keys_rot)
    log_totals = jax.nn.logsumexp(scores, axis=-1)
    softmax_b = jnp.exp(scores - log_totals[..., None]).astype(jnp.bfloat16)
    attended = jnp.einsum(
        "jgqk,kgh->jqgh", softmax_b, values, preferred_element_type=jnp.float32
    ).astype(jnp.bfloat16)
    return (attended, log_totals)


def attend_back(items):
    queries, keys_rot, values, attended, log_totals, attended_cot = items
    scale = queries.shape[-1] ** (-0.5)
    scores = causal_scores(queries, keys_rot)
    softmax_f = jnp.exp(scores - log_totals[..., None])
    softmax_b = softmax_f.astype(jnp.bfloat16)
    value_cot = jnp.einsum(
        "jgqk,jqgh->kgh", softmax_b, attended_cot, preferred_element_type=jnp.float32
    )
    weight_cot = jnp.einsum(
        "jqgh,kgh->jgqk", attended_cot, values, preferred_element_type=jnp.float32
    )
    row_dots = jnp.einsum(
        "jqgh,jqgh->jgq", attended_cot, attended, preferred_element_type=jnp.float32
    )
    score_cot = (softmax_f * (weight_cot - row_dots[..., None])).astype(jnp.bfloat16)
    query_cot = (
        jnp.einsum("jgqk,kgh->jqgh", score_cot, keys_rot, preferred_element_type=jnp.float32)
        * scale
    )
    key_cot = (
        jnp.einsum("jgqk,jqgh->kgh", score_cot, queries, preferred_element_type=jnp.float32) * scale
    )
    return (query_cot, key_cot, value_cot)


def slot_table(route_rows, gate_rows, tok_count):
    hits = (route_rows[:, :, None] == jnp.arange(E, dtype=jnp.int32)[None, None, :]).astype(
        jnp.int32
    )
    per_token = jnp.sum(hits, axis=1, dtype=jnp.int32)
    before = jnp.cumsum(per_token, axis=0, dtype=jnp.int32) - per_token
    position = jnp.sum(hits * before[:, None, :], axis=2, dtype=jnp.int32)
    flat_slot = (route_rows * CAP + position).reshape(-1)
    owner = jnp.broadcast_to(
        jnp.arange(tok_count, dtype=jnp.int32)[:, None], route_rows.shape
    ).reshape(-1)
    slot_token = jnp.full((E * CAP,), tok_count, jnp.int32).at[flat_slot].set(owner)
    slot_weight = jnp.zeros((E * CAP,), jnp.float32).at[flat_slot].set(gate_rows.reshape(-1))
    return (slot_token, slot_weight)


def fetch_experts(w_gate_up, w_down, start_expert, per_turn):
    gate_up_part = w_gate_up[start_expert : start_expert + per_turn].astype(jnp.bfloat16)
    down_part = w_down[start_expert : start_expert + per_turn].astype(jnp.bfloat16)
    return (
        lax.all_gather(gate_up_part, "dp", axis=2, tiled=True),
        lax.all_gather(down_part, "dp", axis=1, tiled=True),
    )


def adamw_update(weight, moment_one, moment_two, gradient, rate, decay):
    new_one = beta_one * moment_one + (1.0 - beta_one) * gradient
    new_two = beta_two * moment_two + (1.0 - beta_two) * gradient * gradient
    corrected_one = new_one / (1.0 - beta_one**STEP)
    corrected_two = new_two / (1.0 - beta_two**STEP)
    new_weight = weight - rate * (
        corrected_one / (jnp.sqrt(corrected_two) + adam_eps) + decay * weight
    )
    return (new_weight, new_one, new_two)


def local(
    block_in,
    cotangent,
    routes,
    gate_weights,
    norm_gains,
    attention_weight,
    output_weight,
    w_gate_up,
    w_down,
    m_gains,
    v_gains,
    attention_first_moment,
    attention_second_moment,
    output_first_moment,
    output_second_moment,
    m_gate_up,
    v_gate_up,
    m_down,
    v_down,
):
    gains_all, attn_all, out_all = (
        lax.all_gather(norm_gains.astype(jnp.bfloat16), "dp", axis=1, tiled=True),
        lax.all_gather(attention_weight.astype(jnp.bfloat16), "dp", axis=1, tiled=True),
        lax.all_gather(output_weight.astype(jnp.bfloat16), "dp", axis=1, tiled=True),
    )
    tok_count = routes.shape[0]
    seq_count = tok_count // SEQ
    width = block_in.shape[1]
    kv_count = attn_all.shape[2] // HEAD_SIZE
    cos_table, sine_table = rope_tables(SEQ, HEAD_SIZE)
    gain_one = gains_all[0].astype(jnp.float32)
    gain_two = gains_all[1].astype(jnp.float32)
    inv_one = lax.rsqrt(jnp.mean(block_in * block_in, axis=1, keepdims=True) + norm_eps)
    normed_one = (block_in * inv_one * gain_one).astype(jnp.bfloat16)
    tokens_one = lax.all_gather(normed_one, "tensor", axis=0, tiled=True)
    projected = jnp.einsum("td,zdc->ztc", tokens_one, attn_all, preferred_element_type=jnp.float32)
    head_vals = projected.reshape(4, seq_count, SEQ, kv_count, HEAD_SIZE)
    queries = (
        rotate(head_vals[0:2], cos_table, sine_table).astype(jnp.bfloat16).transpose(1, 0, 2, 3, 4)
    )
    keys_rot = rotate(head_vals[2], cos_table, sine_table).astype(jnp.bfloat16)
    values = head_vals[3].astype(jnp.bfloat16)
    attended, log_totals = lax.map(attend, (queries, keys_rot, values))
    attended_flat = attended.transpose(1, 0, 2, 3, 4).reshape(2, tok_count, kv_count * HEAD_SIZE)
    partial_value = jnp.einsum(
        "jtc,jdc->td", attended_flat, out_all, preferred_element_type=jnp.float32
    )
    residual = block_in + lax.psum_scatter(partial_value, "tensor", scatter_dimension=0, tiled=True)
    inv_two = lax.rsqrt(jnp.mean(residual * residual, axis=1, keepdims=True) + norm_eps)
    normed_two = (residual * inv_two * gain_two).astype(jnp.bfloat16)
    tokens_two = lax.all_gather(normed_two, "tensor", axis=0, tiled=True)
    slot_token, slot_weight = slot_table(routes, gate_weights, tok_count)
    padded = jnp.concatenate([tokens_two, jnp.zeros((1, width), jnp.bfloat16)], axis=0)
    expert_in = padded[slot_token].reshape(E, CAP, width)
    per_turn = 8
    mixture = jnp.zeros((tok_count + 1, width), jnp.float32)
    saved_acts = []
    for start_expert in range(0, E, per_turn):
        gate_up_g, down_g = fetch_experts(w_gate_up, w_down, start_expert, per_turn)
        inputs = expert_in[start_expert : start_expert + per_turn]
        gate_up = jnp.einsum(
            "ecd,ezdf->zecf", inputs, gate_up_g, preferred_element_type=jnp.float32
        )
        hidden = (jax.nn.silu(gate_up[0]) * gate_up[1]).astype(jnp.bfloat16)
        expert_out = jnp.einsum("ecf,edf->ecd", hidden, down_g, preferred_element_type=jnp.float32)
        slot_rows = slot_token[start_expert * CAP : (start_expert + per_turn) * CAP]
        row_weight = slot_weight[start_expert * CAP : (start_expert + per_turn) * CAP]
        mixture = mixture.at[slot_rows].add(expert_out.reshape(-1, width) * row_weight[:, None])
        saved_acts.append((gate_up, hidden))
    block_out = residual + lax.psum_scatter(
        mixture[:tok_count].astype(jnp.bfloat16), "tensor", scatter_dimension=0, tiled=True
    ).astype(jnp.float32)
    cot_all = lax.all_gather(cotangent, "tensor", axis=0, tiled=True)
    cot_pad = jnp.concatenate([cot_all, jnp.zeros((1, width), jnp.float32)], axis=0)
    slot_cot = (
        (slot_weight[:, None] * cot_pad[slot_token]).astype(jnp.bfloat16).reshape(E, CAP, width)
    )
    back_sum = jnp.zeros((tok_count + 1, width), jnp.float32)
    parts_gate_up = []
    parts_down = []
    for turn_index, start_expert in enumerate(range(0, E, per_turn)):
        gate_up_g, down_g = fetch_experts(w_gate_up, w_down, start_expert, per_turn)
        gate_up, hidden = saved_acts[turn_index]
        gate_vals = gate_up[0]
        up_vals = gate_up[1]
        inputs = expert_in[start_expert : start_expert + per_turn]
        turn_cot = slot_cot[start_expert : start_expert + per_turn]
        down_local = jnp.einsum(
            "ecd,ecf->edf", turn_cot, hidden, preferred_element_type=jnp.float32
        )
        hidden_cot = jnp.einsum(
            "ecd,edf->ecf", turn_cot, down_g, preferred_element_type=jnp.float32
        )
        sigmoid_vals = jax.nn.sigmoid(gate_vals)
        gate_cot = (
            hidden_cot * up_vals * sigmoid_vals * (1.0 + gate_vals * (1.0 - sigmoid_vals))
        ).astype(jnp.bfloat16)
        up_cot = (hidden_cot * gate_vals * sigmoid_vals).astype(jnp.bfloat16)
        both_cot = jnp.stack([gate_cot, up_cot])
        gate_up_local = jnp.einsum(
            "ecd,zecf->ezdf", inputs, both_cot, preferred_element_type=jnp.float32
        )
        input_cot = jnp.einsum(
            "zecf,ezdf->ecd", both_cot, gate_up_g, preferred_element_type=jnp.float32
        )
        slot_rows = slot_token[start_expert * CAP : (start_expert + per_turn) * CAP]
        back_sum = back_sum.at[slot_rows].add(input_cot.reshape(-1, width))
        summed_gate_up, summed_down = (
            lax.psum_scatter(gate_up_local, "dp", scatter_dimension=2, tiled=True),
            lax.psum_scatter(down_local, "dp", scatter_dimension=1, tiled=True),
        )
        parts_gate_up.append(summed_gate_up)
        parts_down.append(summed_down)
    grad_gate_up = jnp.concatenate(parts_gate_up, axis=0)
    grad_down = jnp.concatenate(parts_down, axis=0)
    normed_two_cot = lax.psum_scatter(
        back_sum[:tok_count], "tensor", scatter_dimension=0, tiled=True
    )
    scaled_two = gain_two * normed_two_cot
    residual_cot = (
        cotangent
        + inv_two * scaled_two
        - residual * inv_two**3 * jnp.mean(scaled_two * residual, axis=1, keepdims=True)
    )
    resid_all = lax.all_gather(residual_cot.astype(jnp.bfloat16), "tensor", axis=0, tiled=True)
    out_local = jnp.einsum(
        "td,jtc->jdc", resid_all, attended_flat, preferred_element_type=jnp.float32
    )
    attended_cot = jnp.einsum(
        "td,jdc->jtc", resid_all, out_all, preferred_element_type=jnp.float32
    ).astype(jnp.bfloat16)
    attended_cot = attended_cot.reshape(2, seq_count, SEQ, kv_count, HEAD_SIZE).transpose(
        1, 0, 2, 3, 4
    )
    query_cot, key_cot, value_cot = lax.map(
        attend_back, (queries, keys_rot, values, attended, log_totals, attended_cot)
    )
    query_plain = (
        unrotate(query_cot, cos_table, sine_table)
        .transpose(1, 0, 2, 3, 4)
        .reshape(2, tok_count, kv_count * HEAD_SIZE)
    )
    key_plain = unrotate(key_cot, cos_table, sine_table).reshape(1, tok_count, kv_count * HEAD_SIZE)
    proj_cot = jnp.concatenate(
        [query_plain, key_plain, value_cot.reshape(1, tok_count, kv_count * HEAD_SIZE)], axis=0
    ).astype(jnp.bfloat16)
    attn_local = jnp.einsum("td,ztc->zdc", tokens_one, proj_cot, preferred_element_type=jnp.float32)
    norm_terms = jnp.einsum("ztc,zdc->td", proj_cot, attn_all, preferred_element_type=jnp.float32)
    normed_one_cot = lax.psum_scatter(
        norm_terms.astype(jnp.bfloat16), "tensor", scatter_dimension=0, tiled=True
    ).astype(jnp.float32)
    scaled_one = gain_one * normed_one_cot
    input_grad = (
        residual_cot
        + inv_one * scaled_one
        - block_in * inv_one**3 * jnp.mean(scaled_one * block_in, axis=1, keepdims=True)
    )
    gain_local = jnp.stack(
        [
            jnp.sum(normed_one_cot * block_in * inv_one, axis=0),
            jnp.sum(normed_two_cot * residual * inv_two, axis=0),
        ]
    )
    gain_part, grad_attn, grad_out = (
        lax.psum_scatter(gain_local, "dp", scatter_dimension=1, tiled=True),
        lax.psum_scatter(attn_local, "dp", scatter_dimension=1, tiled=True),
        lax.psum_scatter(out_local, "dp", scatter_dimension=1, tiled=True),
    )
    grad_gains = lax.psum(gain_part, "tensor")
    new_gains, new_m_gains, new_v_gains = adamw_update(
        norm_gains, m_gains, v_gains, grad_gains, rate_gain, 0.0
    )
    new_attn, new_m_attn, new_v_attn = adamw_update(
        attention_weight,
        attention_first_moment,
        attention_second_moment,
        grad_attn,
        rate_matrix,
        decay_matrix,
    )
    new_out, new_m_out, new_v_out = adamw_update(
        output_weight,
        output_first_moment,
        output_second_moment,
        grad_out,
        rate_matrix,
        decay_matrix,
    )
    new_gate_up, new_m_gate_up, new_v_gate_up = adamw_update(
        w_gate_up, m_gate_up, v_gate_up, grad_gate_up, rate_matrix, decay_matrix
    )
    new_down, new_m_down, new_v_down = adamw_update(
        w_down, m_down, v_down, grad_down, rate_matrix, decay_matrix
    )
    return (
        block_out,
        input_grad,
        grad_gains,
        grad_attn,
        grad_out,
        grad_gate_up,
        grad_down,
        new_gains,
        new_attn,
        new_out,
        new_gate_up,
        new_down,
        new_m_gains,
        new_v_gains,
        new_m_attn,
        new_v_attn,
        new_m_out,
        new_v_out,
        new_m_gate_up,
        new_v_gate_up,
        new_m_down,
        new_v_down,
    )


def solution(mesh):
    return jax.shard_map(
        local,
        mesh=mesh,
        in_specs=(
            P(("dp", "tensor"), None),
            P(("dp", "tensor"), None),
            P("dp", None),
            P("dp", None),
            P(None, "dp"),
            P(None, "dp", "tensor"),
            P(None, "dp", "tensor"),
            P(None, None, "dp", "tensor"),
            P(None, "dp", "tensor"),
            P(None, "dp"),
            P(None, "dp"),
            P(None, "dp", "tensor"),
            P(None, "dp", "tensor"),
            P(None, "dp", "tensor"),
            P(None, "dp", "tensor"),
            P(None, None, "dp", "tensor"),
            P(None, None, "dp", "tensor"),
            P(None, "dp", "tensor"),
            P(None, "dp", "tensor"),
        ),
        out_specs=(
            P(("dp", "tensor"), None),
            P(("dp", "tensor"), None),
            P(None, "dp"),
            P(None, "dp", "tensor"),
            P(None, "dp", "tensor"),
            P(None, None, "dp", "tensor"),
            P(None, "dp", "tensor"),
            P(None, "dp"),
            P(None, "dp", "tensor"),
            P(None, "dp", "tensor"),
            P(None, None, "dp", "tensor"),
            P(None, "dp", "tensor"),
            P(None, "dp"),
            P(None, "dp"),
            P(None, "dp", "tensor"),
            P(None, "dp", "tensor"),
            P(None, "dp", "tensor"),
            P(None, "dp", "tensor"),
            P(None, None, "dp", "tensor"),
            P(None, None, "dp", "tensor"),
            P(None, "dp", "tensor"),
            P(None, "dp", "tensor"),
        ),
        check_vma=False,
    )
```

profile of v0, /device:TPU:0, one launch (start us, length us, event | category | flops | bytes accessed | tf_op | source)
XLA Modules:
  0.0 941.3 jit_solution(5812253227274895094)
XLA Ops:
  34.1 16.2 %all-gather.10.cloned.1.call-done = bf16[512,1024]{1,0:T(8,128)(2,1)} async-done(((bf16[128,1024]{1,0:T(8,128)(2,1)}), bf16[512,1024]{1,0:T(8,128)(2,1)}) %all-gather.10.cloned.1.call-update) | async-done | bytes 1048592 | tf_op jit(solution)/shard_map/all_gather | solution.py:174
  50.3 25.3 %all-gather.12.cloned.1.call-done = bf16[4,1024,128]{1,2,0:T(8,128)(2,1)} async-done(((bf16[4,128,128]{1,2,0:T(8,128)(2,1)}), bf16[4,1024,128]{1,2,0:T(8,128)(2,1)}) %all-gather.12.cloned.1.call-update) | async-done | bytes 1048592 | tf_op jit(solution)/shard_map/all_gather | solution.py:162
  86.5 43.2 %reduce-scatter.14.cloned.1.call-done = f32[128,1024]{1,0:T(8,128)} async-done(((f32[512,1024]{1,0:T(8,128)}), f32[128,1024]{1,0:T(8,128)}) %reduce-scatter.14.cloned.1.call-update) | async-done | bytes 524304 | tf_op jit(solution)/shard_map/reduce_scatter | solution.py:187
  139.9 15.5 %scatter_custom_fusion = s32[4608]{0:T(1024)S(1)} fusion(s32[4096]{0:T(1024)S(1)} %bitcast.271, s32[4096]{0:T(1024)S(1)} %reshape.349, s32[]{:T(128)} %constant.51.clone.1), kind=kCustom, calls=%fused_computation.145 | custom fusion | bytes 18436 | tf_op jit(solution)/shard_map/scatter | solution.py:114
  155.8 16.0 %scatter_custom_fusion.1 = f32[4608]{0:T(1024)S(1)} fusion(s32[4096]{0:T(1024)S(1)} %bitcast.272, f32[4096]{0:T(1024)S(1)} %reshape.357, f32[]{:T(128)} %constant.43.clone.1), kind=kCustom, calls=%fused_computation.143 | custom fusion | bytes 18436 | tf_op jit(solution)/shard_map/scatter | solution.py:115
  177.7 15.2 %gather_fusion.1 = f32[4608,1024]{1,0:T(8,128)} fusion(f32[513,1024]{1,0:T(8,128)S(1)} %concatenate.53, s32[5120]{0:T(1024)S(1)} %pad_clamp_fusion), kind=kCustom, calls=%fused_computation.1 | custom fusion | bytes 37767168 | tf_op jit(solution)/shard_map/gather | solution.py:215
  207.0 14.9 %gather_fusion = bf16[4608,1024]{1,0:T(8,128)(2,1)} fusion(bf16[513,1024]{1,0:T(8,128)(2,1)S(1)} %concatenate.52, s32[5120]{0:T(1024)S(1)} %pad_clamp_fusion), kind=kCustom, calls=%fused_computation | custom fusion | bytes 18892800 | tf_op jit(solution)/shard_map/gather | solution.py:193
  230.6 12.5 %all-gather.16.cloned.1.call-done = bf16[8,2,1024,128]{3,2,1,0:T(8,128)(2,1)} async-done(((bf16[8,2,128,128]{3,2,1,0:T(8,128)(2,1)}), bf16[8,2,1024,128]{3,2,1,0:T(8,128)(2,1)}) %all-gather.16.cloned.1.call-update) | async-done | bytes 4194320 | tf_op jit(solution)/shard_map/all_gather | solution.py:123
  248.1 25.3 %all-gather.18.cloned.1.call-done = bf16[8,1024,128]{2,1,0:T(8,128)(2,1)} async-done(((bf16[8,128,128]{2,1,0:T(8,128)(2,1)}), bf16[8,1024,128]{2,1,0:T(8,128)(2,1)}) %all-gather.18.cloned.1.call-update) | async-done | bytes 2097168 | tf_op jit(solution)/shard_map/all_gather | solution.py:124
  283.4 24.2 %scatter_custom_fusion.4 = f32[513,1024]{1,0:T(8,128)S(1)} fusion(s32[2304]{0:T(1024)S(1)} %get-tuple-element.209, f32[2304,1024]{1,0:T(8,128)} %bitcast.236, f32[]{:T(128)} %constant.43.clone.1), kind=kCustom, calls=%fused_computation.65 | custom fusion | flops 2359296 | bytes 2101760 | tf_op jit(solution)/shard_map/scatter-add | solution.py:246
  318.9 23.9 %all-gather.22.cloned.1.call-done = bf16[8,1024,128]{2,1,0:T(8,128)(2,1)} async-done(((bf16[8,128,128]{2,1,0:T(8,128)(2,1)}), bf16[8,1024,128]{2,1,0:T(8,128)(2,1)}) %all-gather.22.cloned.1.call-update) | async-done | bytes 2097168 | tf_op jit(solution)/shard_map/all_gather | solution.py:124
  354.1 24.3 %scatter_fusion.1 = f32[513,1024]{1,0:T(8,128)S(1)} fusion(f32[513,1024]{1,0:T(8,128)S(1)} %scatter_custom_fusion.4, s32[2304]{0:T(1024)S(1)} %get-tuple-element.208, f32[2304,1024]{1,0:T(8,128)} %bitcast.233), kind=kCustom, calls=%fused_computation.7 | custom fusion | flops 2359296 | bytes 28320768 | tf_op jit(solution)/shard_map/scatter-add | solution.py:246
  387.2 24.2 %scatter_custom_fusion.2 = f32[513,1024]{1,0:T(8,128)S(1)} fusion(s32[2304]{0:T(1024)S(1)} %get-tuple-element.209, f32[2304,1024]{1,0:T(8,128)} %bitcast_multiply_fusion.1, f32[]{:T(128)} %constant.43.clone.1), kind=kCustom, calls=%fused_computation.67 | custom fusion | flops 2359296 | bytes 2101760 | tf_op jit(solution)/shard_map/scatter-add | solution.py:207
  419.0 24.1 %scatter_fusion = f32[513,1024]{1,0:T(8,128)S(1)} fusion(f32[513,1024]{1,0:T(8,128)S(1)} %scatter_custom_fusion.2, s32[2304]{0:T(1024)S(1)} %get-tuple-element.208, f32[2304,1024]{1,0:T(8,128)} %bitcast_multiply_fusion), kind=kCustom, calls=%fused_computation.5 | custom fusion | flops 2359296 | bytes 28320768 | tf_op jit(solution)/shard_map/scatter-add | solution.py:207
  445.8 26.1 %reduce-scatter.16.cloned.1.call-done = bf16[128,1024]{1,0:T(8,128)(2,1)} async-done(((bf16[512,1024]{1,0:T(8,128)(2,1)}), bf16[128,1024]{1,0:T(8,128)(2,1)}) %reduce-scatter.16.cloned.1.call-update) | async-done | bytes 262160 | tf_op jit(solution)/shard_map/reduce_scatter | solution.py:209
  474.5 26.4 %all-gather.26.cloned.1.call-done = bf16[512,1024]{1,0:T(8,128)(2,1)} async-done(((bf16[128,1024]{1,0:T(8,128)(2,1)}), bf16[512,1024]{1,0:T(8,128)(2,1)}) %all-gather.26.cloned.1.call-update) | async-done | bytes 1048592 | tf_op jit(solution)/shard_map/all_gather | solution.py:264
  573.0 18.4 %reduce-scatter.30.cloned.1.call-done = f32[8,128,128]{2,1,0:T(8,128)} async-done(((f32[8,1024,128]{2,1,0:T(8,128)}), f32[8,128,128]{2,1,0:T(8,128)}) %reduce-scatter.30.cloned.1.call-update) | async-done | bytes 524304 | tf_op jit(solution)/shard_map/reduce_scatter | solution.py:249
  592.4 53.3 %reduce-scatter.32.cloned.1.call-done = f32[8,128,128]{2,1,0:T(8,128)} async-done(((f32[8,1024,128]{2,1,0:T(8,128)}), f32[8,128,128]{2,1,0:T(8,128)}) %reduce-scatter.32.cloned.1.call-update) | async-done | bytes 524304 | tf_op jit(solution)/shard_map/reduce_scatter | solution.py:249
  651.0 34.3 %reduce-scatter.24.cloned.1.call-done = f32[2,128,128]{1,2,0:T(8,128)} async-done(((f32[2,1024,128]{1,2,0:T(8,128)}), f32[2,128,128]{1,2,0:T(8,128)}) %reduce-scatter.24.cloned.1.call-update) | async-done | bytes 131088 | tf_op jit(solution)/shard_map/reduce_scatter | solution.py:306
  692.6 29.8 %reduce-scatter.34.cloned.1.call-done = f32[128,2]{1,0:T(8,128)} async-done(((f32[1024,2]{1,0:T(8,128)}), f32[128,2]{1,0:T(8,128)}) %reduce-scatter.34.cloned.1.call-update) | async-done | bytes 1040
  723.3 11.7 %psum.7 = f32[2,128]{1,0:T(2,128)S(1)} all-reduce(f32[2,128]{1,0:T(2,128)S(1)} %copy.266), channel_id=1, replica_groups=mesh['dp'=8,'tensor'=4] {'tensor'}, use_global_device_ids=true, to_apply=%region_23.24 | all-reduce | flops 256 | bytes 2048 | tf_op jit(solution)/shard_map/psum | solution.py:308
  735.6 31.7 %reduce-scatter.22.cloned.1.call-done = f32[4,128,128]{1,2,0:T(8,128)} async-done(((f32[4,1024,128]{1,2,0:T(8,128)}), f32[4,128,128]{1,2,0:T(8,128)}) %reduce-scatter.22.cloned.1.call-update) | async-done | bytes 262160 | tf_op jit(solution)/shard_map/reduce_scatter | solution.py:305
  771.8 70.2 %reduce-scatter.26.cloned.1.call-done = f32[8,2,128,128]{2,3,1,0:T(8,128)} async-done(((f32[8,2,1024,128]{2,3,1,0:T(8,128)}), f32[8,2,128,128]{2,3,1,0:T(8,128)}) %reduce-scatter.26.cloned.1.call-update) | async-done | bytes 1048592 | tf_op jit(solution)/shard_map/reduce_scatter | solution.py:248
  843.4 73.3 %reduce-scatter.28.cloned.1.call-done = f32[8,2,128,128]{2,3,1,0:T(8,128)} async-done(((f32[8,2,1024,128]{2,3,1,0:T(8,128)}), f32[8,2,128,128]{2,3,1,0:T(8,128)}) %reduce-scatter.28.cloned.1.call-update) | async-done | bytes 1048592 | tf_op jit(solution)/shard_map/reduce_scatter | solution.py:248
  (333 shorter events, 245.6 us)
Async XLA Ops:
  7.2 43.1 %all-gather.10.cloned.1.call-start = ((), (), s32[]{:S(2)}) async-start(), calls=%async_computation.11 | async-start | bytes 1310720 | tf_op jit(solution)/shard_map/all_gather | solution.py:174
  18.2 113.1 %copy-start.63 = (f32[1,1024]{1,0:T(1,128)}, f32[1,1024]{1,0:T(1,128)S(1)}, u32[]{:S(2)}) copy-start(f32[1,1024]{1,0:T(1,128)S(1)} %get-tuple-element.210) | copy-start | bytes 12292
  21.8 53.8 %all-gather.12.cloned.1.call-start = ((), (), s32[]{:S(2)}) async-start(), calls=%async_computation.12 | async-start | bytes 1179648 | tf_op jit(solution)/shard_map/all_gather | solution.py:162
  23.7 105.9 %reduce-scatter.14.cloned.1.call-start = ((), (), s32[]{:S(2)}) async-start(), calls=%async_computation.13 | async-start | bytes 2621440 | tf_op jit(solution)/shard_map/reduce_scatter | solution.py:187
  85.8 90.1 %all-gather.24.cloned.1.call-start = ((), (), s32[]{:S(2)}) async-start(), calls=%async_computation.20 | async-start | bytes 2621440 | tf_op jit(solution)/shard_map/all_gather | solution.py:212
  86.4 119.2 %all-gather.14.cloned.1.call-start = ((), (), s32[]{:S(2)}) async-start(), calls=%async_computation.14 | async-start | bytes 1310720 | tf_op jit(solution)/shard_map/all_gather | solution.py:190
  132.7 110.4 %all-gather.16.cloned.1.call-start = ((), (), s32[]{:S(2)}) async-start(), calls=%async_computation.15 | async-start | bytes 4718592 | tf_op jit(solution)/shard_map/all_gather | solution.py:123
  134.0 139.4 %all-gather.18.cloned.1.call-start = ((), (), s32[]{:S(2)}) async-start(), calls=%async_computation.16 | async-start | bytes 2359296 | tf_op jit(solution)/shard_map/all_gather | solution.py:124
  136.2 176.2 %all-gather.20.cloned.1.call-start = ((), (), s32[]{:S(2)}) async-start(), calls=%async_computation.17 | async-start | bytes 4718592 | tf_op jit(solution)/shard_map/all_gather | solution.py:123
  137.0 205.8 %all-gather.22.cloned.1.call-start = ((), (), s32[]{:S(2)}) async-start(), calls=%async_computation.18 | async-start | bytes 2359296 | tf_op jit(solution)/shard_map/all_gather | solution.py:124
  137.7 306.7 %reduce-scatter.18.cloned.1.call-start = ((), (), s32[]{:S(2)}) async-start(), calls=%async_computation.21 | async-start | bytes 2621440 | tf_op jit(solution)/shard_map/reduce_scatter | solution.py:255
  379.9 91.9 %reduce-scatter.16.cloned.1.call-start = ((), (), s32[]{:S(2)}) async-start(), calls=%async_computation.19 | async-start | bytes 1310720 | tf_op jit(solution)/shard_map/reduce_scatter | solution.py:209
  444.4 56.5 %all-gather.26.cloned.1.call-start = ((), (), s32[]{:S(2)}) async-start(), calls=%async_computation.22 | async-start | bytes 1310720 | tf_op jit(solution)/shard_map/all_gather | solution.py:264
  474.2 64.3 %reduce-scatter.20.cloned.1.call-start = ((), (), s32[]{:S(2)}) async-start(), calls=%async_computation.23 | async-start | bytes 1310720 | tf_op jit(solution)/shard_map/reduce_scatter | solution.py:288
  511.7 79.7 %reduce-scatter.30.cloned.1.call-start = ((), (), s32[]{:S(2)}) async-start(), calls=%async_computation.28 | async-start | bytes 4718592 | tf_op jit(solution)/shard_map/reduce_scatter | solution.py:249
  518.2 127.5 %reduce-scatter.32.cloned.1.call-start = ((), (), s32[]{:S(2)}) async-start(), calls=%async_computation.29 | async-start | bytes 4718592 | tf_op jit(solution)/shard_map/reduce_scatter | solution.py:249
  525.7 159.6 %reduce-scatter.24.cloned.1.call-start = ((), (), s32[]{:S(2)}) async-start(), calls=%async_computation.25 | async-start | bytes 1179648 | tf_op jit(solution)/shard_map/reduce_scatter | solution.py:306
  528.3 194.0 %reduce-scatter.34.cloned.1.call-start = ((), (), s32[]{:S(2)}) async-start(), calls=%async_computation.30 | async-start | bytes 589824
  541.3 226.0 %reduce-scatter.22.cloned.1.call-start = ((), (), s32[]{:S(2)}) async-start(), calls=%async_computation.24 | async-start | bytes 2359296 | tf_op jit(solution)/shard_map/reduce_scatter | solution.py:305
  543.4 298.6 %reduce-scatter.26.cloned.1.call-start = ((), (), s32[]{:S(2)}) async-start(), calls=%async_computation.26 | async-start | bytes 9437184 | tf_op jit(solution)/shard_map/reduce_scatter | solution.py:248
  552.1 364.6 %reduce-scatter.28.cloned.1.call-start = ((), (), s32[]{:S(2)}) async-start(), calls=%async_computation.27 | async-start | bytes 9437184 | tf_op jit(solution)/shard_map/reduce_scatter | solution.py:248
  650.9 84.0 %copy-start.73 = (f32[2,128]{1,0:T(2,128)S(1)}, f32[2,128]{1,0:T(2,128)}, u32[]{:S(2)}) copy-start(f32[2,128]{1,0:T(2,128)} %param.23) | copy-start | bytes 3076
  651.0 116.3 %copy-start.24 = (f32[4,128,128]{1,2,0:T(8,128)S(1)}, f32[4,128,128]{1,2,0:T(8,128)}, u32[]{:S(2)}) copy-start(f32[4,128,128]{1,2,0:T(8,128)} %copy-done.23) | copy-start | bytes 786436
  735.0 108.4 %copy-start.72 = (f32[2,128]{1,0:T(2,128)}, f32[2,128]{1,0:T(2,128)S(1)}, u32[]{:S(2)}) copy-start(f32[2,128]{1,0:T(2,128)S(1)} %psum.7) | copy-start | bytes 3076
  (73 other events, 880.6 us)
Sparse Core Ops, SparseCore 0:
  21.9 28.2 all-gather.9
  52.7 22.8 all-gather.11
  85.9 43.6 reduce-scatter.13
  131.0 44.8 all-gather.23
  177.9 26.7 all-gather.13
  207.1 35.9 all-gather.15
  245.6 27.7 all-gather.17
  275.9 36.5 all-gather.19
  315.0 27.7 all-gather.21
  380.1 43.5 reduce-scatter.17
  444.5 27.3 reduce-scatter.15
  474.4 26.4 all-gather.25
  511.8 26.6 reduce-scatter.19
  541.7 49.5 reduce-scatter.29
  594.6 51.0 reduce-scatter.31
  649.3 35.9 reduce-scatter.23
  688.2 34.0 reduce-scatter.33
  726.1 41.1 reduce-scatter.21
  770.7 71.2 reduce-scatter.25
  845.3 71.2 reduce-scatter.27
where the time goes:
time: 950 us; the launch traced here: 941 us
  waiting for transfers between devices  531 us (56%)
  other arithmetic  148 us (16%)
  local copies, waits for them, and re-layouts  130 us (14%)
  matrix products  83.7 us (9%)
  blocking collectives  31.8 us (3%)
  between operations  15.7 us (2%)
    reduce_scatter x2, waiting for transfers between devices, local(): lax.psum_scatter(gate_up_local, 'dp', scatter_dimension=2, tiled=True)  144 us
    reduce_scatter x2, waiting for transfers between devices, local(): lax.psum_scatter(down_local, 'dp', scatter_dimension=1, tiled=True)  71.7 us
    all_gather x2, waiting for transfers between devices, fetch_experts(): lax.all_gather(down_part, 'dp', axis=1, tiled=True)  49.2 us
    scatter-add x2, other arithmetic, local(): back_sum = back_sum.at[slot_rows].add(input_cot.reshape(-1, width))  48.5 us
    scatter-add x2, other arithmetic, local(): mixture.at[slot_rows]  48.4 us
    unnamed x180, local copies, waits for them, and re-layouts  43.3 us
    reduce_scatter x1, waiting for transfers between devices, local(): lax.psum_scatter(partial_value, 'tensor', scatter_dimension=0, tiled=True)  43.2 us
    reduce_scatter x1, waiting for transfers between devices, local(): lax.psum_scatter(out_local, 'dp', scatter_dimension=1, tiled=True)  34.3 us
  transfers between devices with their start and end apart: 20, of which 18 were waited for; matrix products, arithmetic and copies ran while one was open for 29% of the time, Pallas kernels for 0%

commit v1 on v0

--- a/solution.py
+++ b/solution.py
@@ -121,7 +121,9 @@
     down_part = w_down[start_expert : start_expert + per_turn].astype(jnp.bfloat16)
     return (
         lax.all_gather(gate_up_part, "dp", axis=2, tiled=True),
-        lax.all_gather(down_part, "dp", axis=1, tiled=True),
+        jnp.concatenate(
+            lax.all_to_all(jnp.stack([down_part] * lax.axis_size("dp")), "dp", 0, 0), axis=1
+        ),
     )
 
 

time: 950 us -> 916 us (0.964)
  waiting for transfers between devices: 531 us -> 484 us
    all_gather x2 -> x0, waiting for transfers between devices: 49.2 us -> none  [fetch_experts(): lax.all_gather(down_part, 'dp', axis=1, tiled=True)]
    all_to_all x0 -> x2, waiting for transfers between devices: none -> 24.4 us  [fetch_experts(): lax.all_to_all(jnp.stack([down_part] * lax.axis_size('dp')), 'dp', 0, 0)]
    all_gather x2, waiting for transfers between devices: 17.5 us -> 0.02 us  [fetch_experts(): lax.all_gather(gate_up_part, 'dp', axis=2, tiled=True)]
    unnamed x180 -> x186, local copies, waits for them, and re-layouts: 43.3 us -> 44.2 us
    unnamed x21 -> x19, waiting for transfers between devices: 32 us -> 31.3 us
  transfers between devices with their start and end apart: 20 -> 20, of which waited for: 18 -> 14; matrix products, arithmetic and copies ran while one was open for 29% -> 30% of each run, Pallas kernels for 0% -> 0%
where the time goes in v1:
time: 916 us; the launch traced here: 906 us
  waiting for transfers between devices  484 us (53%)
  other arithmetic  148 us (16%)
  local copies, waits for them, and re-layouts  138 us (15%)
  matrix products  79.1 us (9%)
  blocking collectives  31.8 us (3%)
  between operations  15.8 us (2%)
  starting transfers between devices  9.39 us (1%)
    reduce_scatter x2, waiting for transfers between devices, local(): lax.psum_scatter(gate_up_local, 'dp', scatter_dimension=2, tiled=True)  143 us
    reduce_scatter x2, waiting for transfers between devices, local(): lax.psum_scatter(down_local, 'dp', scatter_dimension=1, tiled=True)  71.8 us
    scatter-add x2, other arithmetic, local(): back_sum = back_sum.at[slot_rows].add(input_cot.reshape(-1, width))  48.4 us
    scatter-add x2, other arithmetic, local(): mixture.at[slot_rows]  48.4 us
    unnamed x186, local copies, waits for them, and re-layouts  44.2 us
    reduce_scatter x1, waiting for transfers between devices, local(): lax.psum_scatter(partial_value, 'tensor', scatter_dimension=0, tiled=True)  43.2 us
    reduce_scatter x1, waiting for transfers between devices, local(): lax.psum_scatter(out_local, 'dp', scatter_dimension=1, tiled=True)  34.3 us
    reduce_scatter x1, waiting for transfers between devices, local(): lax.psum_scatter(attn_local, 'dp', scatter_dimension=1, tiled=True)  31.6 us
  transfers between devices with their start and end apart: 20, of which 14 were waited for; matrix products, arithmetic and copies ran while one was open for 30% of the time, Pallas kernels for 0%

profile of v1, /device:TPU:0, one launch (start us, length us, event | category | flops | bytes accessed | tf_op | source)
XLA Modules:
  0.0 906.2 jit_solution(16293254791257228627)
XLA Ops:
  8.0 10.3 %all_gather.29 = bf16[2,1024]{1,0:T(2,128)(2,1)S(1)} all-gather(bf16[2,128]{1,0:T(2,128)(2,1)S(1)} %convert_element_type.103), channel_id=1, replica_groups=mesh['dp'=8,'tensor'=4] {'dp'}, dimensions={1}, use_global_device_ids=true | all-gather | bytes 4608 | tf_op jit(solution)/shard_map/all_gather | solution.py:163
  34.1 16.1 %all-gather.8.cloned.1.call-done = bf16[512,1024]{1,0:T(8,128)(2,1)} async-done(((bf16[128,1024]{1,0:T(8,128)(2,1)}), bf16[512,1024]{1,0:T(8,128)(2,1)}) %all-gather.8.cloned.1.call-update) | async-done | bytes 1048592 | tf_op jit(solution)/shard_map/all_gather | solution.py:176
  50.3 25.3 %all-gather.10.cloned.1.call-done = bf16[4,1024,128]{1,2,0:T(8,128)(2,1)} async-done(((bf16[4,128,128]{1,2,0:T(8,128)(2,1)}), bf16[4,1024,128]{1,2,0:T(8,128)(2,1)}) %all-gather.10.cloned.1.call-update) | async-done | bytes 1048592 | tf_op jit(solution)/shard_map/all_gather | solution.py:164
  86.5 43.2 %reduce-scatter.14.cloned.1.call-done = f32[128,1024]{1,0:T(8,128)} async-done(((f32[512,1024]{1,0:T(8,128)}), f32[128,1024]{1,0:T(8,128)}) %reduce-scatter.14.cloned.1.call-update) | async-done | bytes 524304 | tf_op jit(solution)/shard_map/reduce_scatter | solution.py:189
  143.2 24.4 %all-to-all-done = bf16[8,8,128,128]{3,2,1,0:T(8,128)(2,1)S(1)} async-done(((bf16[8,8,128,128]{3,2,1,0:T(8,128)(2,1)}), bf16[8,8,128,128]{3,2,1,0:T(8,128)(2,1)S(1)}, u32[]{:S(2)}, u32[]{:S(2)}) %all-to-all-start) | async-done | bytes 2097184 | tf_op jit(solution)/shard_map/all_to_all | solution.py:125
  175.0 15.5 %scatter_custom_fusion = s32[4608]{0:T(1024)S(1)} fusion(s32[4096]{0:T(1024)S(1)} %bitcast.280, s32[4096]{0:T(1024)S(1)} %reshape.373, s32[]{:T(128)} %constant.51.clone.1), kind=kCustom, calls=%fused_computation.145 | custom fusion | bytes 18436 | tf_op jit(solution)/shard_map/scatter | solution.py:114
  190.5 16.0 %scatter_custom_fusion.1 = f32[4608]{0:T(1024)S(1)} fusion(s32[4096]{0:T(1024)S(1)} %bitcast.281, f32[4096]{0:T(1024)S(1)} %reshape.381, f32[]{:T(128)} %constant.43.clone.1), kind=kCustom, calls=%fused_computation.143 | custom fusion | bytes 18436 | tf_op jit(solution)/shard_map/scatter | solution.py:115
  212.9 15.2 %gather_fusion.1 = f32[4608,1024]{1,0:T(8,128)} fusion(f32[513,1024]{1,0:T(8,128)S(1)} %concatenate.53, s32[5120]{0:T(1024)S(1)} %pad_clamp_fusion), kind=kCustom, calls=%fused_computation.1 | custom fusion | bytes 37767168 | tf_op jit(solution)/shard_map/gather | solution.py:217
  242.3 14.9 %gather_fusion = bf16[4608,1024]{1,0:T(8,128)(2,1)} fusion(bf16[513,1024]{1,0:T(8,128)(2,1)S(1)} %concatenate.52, s32[5120]{0:T(1024)S(1)} %pad_clamp_fusion), kind=kCustom, calls=%fused_computation | custom fusion | bytes 18892800 | tf_op jit(solution)/shard_map/gather | solution.py:195
  279.4 24.0 %scatter_custom_fusion.4 = f32[513,1024]{1,0:T(8,128)S(1)} fusion(s32[2304]{0:T(1024)S(1)} %get-tuple-element.209, f32[2304,1024]{1,0:T(8,128)} %bitcast.240, f32[]{:T(128)} %constant.43.clone.1), kind=kCustom, calls=%fused_computation.65 | custom fusion | flops 2359296 | bytes 2101760 | tf_op jit(solution)/shard_map/scatter-add | solution.py:248
  318.9 24.3 %scatter_fusion.1 = f32[513,1024]{1,0:T(8,128)S(1)} fusion(f32[513,1024]{1,0:T(8,128)S(1)} %scatter_custom_fusion.4, s32[2304]{0:T(1024)S(1)} %get-tuple-element.208, f32[2304,1024]{1,0:T(8,128)} %bitcast.237), kind=kCustom, calls=%fused_computation.7 | custom fusion | flops 2359296 | bytes 28320768 | tf_op jit(solution)/shard_map/scatter-add | solution.py:248
  352.0 24.2 %scatter_custom_fusion.2 = f32[513,1024]{1,0:T(8,128)S(1)} fusion(s32[2304]{0:T(1024)S(1)} %get-tuple-element.209, f32[2304,1024]{1,0:T(8,128)} %bitcast_multiply_fusion.1, f32[]{:T(128)} %constant.43.clone.1), kind=kCustom, calls=%fused_computation.67 | custom fusion | flops 2359296 | bytes 2101760 | tf_op jit(solution)/shard_map/scatter-add | solution.py:209
  383.8 24.1 %scatter_fusion = f32[513,1024]{1,0:T(8,128)S(1)} fusion(f32[513,1024]{1,0:T(8,128)S(1)} %scatter_custom_fusion.2, s32[2304]{0:T(1024)S(1)} %get-tuple-element.208, f32[2304,1024]{1,0:T(8,128)} %bitcast_multiply_fusion), kind=kCustom, calls=%fused_computation.5 | custom fusion | flops 2359296 | bytes 28320768 | tf_op jit(solution)/shard_map/scatter-add | solution.py:209
  410.5 26.3 %reduce-scatter.16.cloned.1.call-done = bf16[128,1024]{1,0:T(8,128)(2,1)} async-done(((bf16[512,1024]{1,0:T(8,128)(2,1)}), bf16[128,1024]{1,0:T(8,128)(2,1)}) %reduce-scatter.16.cloned.1.call-update) | async-done | bytes 262160 | tf_op jit(solution)/shard_map/reduce_scatter | solution.py:211
  439.5 26.3 %all-gather.20.cloned.1.call-done = bf16[512,1024]{1,0:T(8,128)(2,1)} async-done(((bf16[128,1024]{1,0:T(8,128)(2,1)}), bf16[512,1024]{1,0:T(8,128)(2,1)}) %all-gather.20.cloned.1.call-update) | async-done | bytes 1048592 | tf_op jit(solution)/shard_map/all_gather | solution.py:266
  493.4 10.1 %reduce-scatter.20.cloned.1.call-done = bf16[128,1024]{1,0:T(8,128)(2,1)} async-done(((bf16[512,1024]{1,0:T(8,128)(2,1)}), bf16[128,1024]{1,0:T(8,128)(2,1)}) %reduce-scatter.20.cloned.1.call-update) | async-done | bytes 262160 | tf_op jit(solution)/shard_map/reduce_scatter | solution.py:290
  537.9 18.4 %reduce-scatter.30.cloned.1.call-done = f32[8,128,128]{2,1,0:T(8,128)} async-done(((f32[8,1024,128]{2,1,0:T(8,128)}), f32[8,128,128]{2,1,0:T(8,128)}) %reduce-scatter.30.cloned.1.call-update) | async-done | bytes 524304 | tf_op jit(solution)/shard_map/reduce_scatter | solution.py:251
  557.4 53.4 %reduce-scatter.32.cloned.1.call-done = f32[8,128,128]{2,1,0:T(8,128)} async-done(((f32[8,1024,128]{2,1,0:T(8,128)}), f32[8,128,128]{2,1,0:T(8,128)}) %reduce-scatter.32.cloned.1.call-update) | async-done | bytes 524304 | tf_op jit(solution)/shard_map/reduce_scatter | solution.py:251
  616.0 34.3 %reduce-scatter.24.cloned.1.call-done = f32[2,128,128]{1,2,0:T(8,128)} async-done(((f32[2,1024,128]{1,2,0:T(8,128)}), f32[2,128,128]{1,2,0:T(8,128)}) %reduce-scatter.24.cloned.1.call-update) | async-done | bytes 131088 | tf_op jit(solution)/shard_map/reduce_scatter | solution.py:308
  657.6 29.8 %reduce-scatter.34.cloned.1.call-done = f32[128,2]{1,0:T(8,128)} async-done(((f32[1024,2]{1,0:T(8,128)}), f32[128,2]{1,0:T(8,128)}) %reduce-scatter.34.cloned.1.call-update) | async-done | bytes 1040
  688.3 11.7 %psum.7 = f32[2,128]{1,0:T(2,128)S(1)} all-reduce(f32[2,128]{1,0:T(2,128)S(1)} %copy.270), channel_id=1, replica_groups=mesh['dp'=8,'tensor'=4] {'tensor'}, use_global_device_ids=true, to_apply=%region_23.24 | all-reduce | flops 256 | bytes 2048 | tf_op jit(solution)/shard_map/psum | solution.py:310
  700.6 31.6 %reduce-scatter.22.cloned.1.call-done = f32[4,128,128]{1,2,0:T(8,128)} async-done(((f32[4,1024,128]{1,2,0:T(8,128)}), f32[4,128,128]{1,2,0:T(8,128)}) %reduce-scatter.22.cloned.1.call-update) | async-done | bytes 262160 | tf_op jit(solution)/shard_map/reduce_scatter | solution.py:307
  736.9 70.0 %reduce-scatter.26.cloned.1.call-done = f32[8,2,128,128]{2,3,1,0:T(8,128)} async-done(((f32[8,2,1024,128]{2,3,1,0:T(8,128)}), f32[8,2,128,128]{2,3,1,0:T(8,128)}) %reduce-scatter.26.cloned.1.call-update) | async-done | bytes 1048592 | tf_op jit(solution)/shard_map/reduce_scatter | solution.py:250
  808.2 73.3 %reduce-scatter.28.cloned.1.call-done = f32[8,2,128,128]{2,3,1,0:T(8,128)} async-done(((f32[8,2,1024,128]{2,3,1,0:T(8,128)}), f32[8,2,128,128]{2,3,1,0:T(8,128)}) %reduce-scatter.28.cloned.1.call-update) | async-done | bytes 1048592 | tf_op jit(solution)/shard_map/reduce_scatter | solution.py:250
  (341 shorter events, 227.4 us)
Async XLA Ops:
  7.2 43.1 %all-gather.8.cloned.1.call-start = ((), (), s32[]{:S(2)}) async-start(), calls=%async_computation.13 | async-start | bytes 1310720 | tf_op jit(solution)/shard_map/all_gather | solution.py:176
  18.2 113.2 %copy-start.66 = (f32[1,1024]{1,0:T(1,128)}, f32[1,1024]{1,0:T(1,128)S(1)}, u32[]{:S(2)}) copy-start(f32[1,1024]{1,0:T(1,128)S(1)} %get-tuple-element.210) | copy-start | bytes 12292
  21.8 53.8 %all-gather.10.cloned.1.call-start = ((), (), s32[]{:S(2)}) async-start(), calls=%async_computation.14 | async-start | bytes 1179648 | tf_op jit(solution)/shard_map/all_gather | solution.py:164
  23.7 105.9 %reduce-scatter.14.cloned.1.call-start = ((), (), s32[]{:S(2)}) async-start(), calls=%async_computation.15 | async-start | bytes 2621440 | tf_op jit(solution)/shard_map/reduce_scatter | solution.py:189
  85.8 125.3 %all-gather.18.cloned.1.call-start = ((), (), s32[]{:S(2)}) async-start(), calls=%async_computation.20 | async-start | bytes 2621440 | tf_op jit(solution)/shard_map/all_gather | solution.py:214
  86.4 154.6 %all-gather.12.cloned.1.call-start = ((), (), s32[]{:S(2)}) async-start(), calls=%async_computation.16 | async-start | bytes 1310720 | tf_op jit(solution)/shard_map/all_gather | solution.py:192
  132.7 133.0 %all-gather.14.cloned.1.call-start = ((), (), s32[]{:S(2)}) async-start(), calls=%async_computation.17 | async-start | bytes 4718592 | tf_op jit(solution)/shard_map/all_gather | solution.py:123
  137.2 30.4 %all-to-all-start = ((bf16[8,8,128,128]{3,2,1,0:T(8,128)(2,1)}), bf16[8,8,128,128]{3,2,1,0:T(8,128)(2,1)S(1)}, u32[]{:S(2)}, u32[]{:S(2)}) async-start(bf16[8,8,128,128]{3,2,1,0:T(8,128)(2,1)} %stack.22), calls=%async_computation.1 | async-start | bytes 4194304 | tf_op jit(solution)/shard_map/all_to_all | solution.py:125
  141.0 162.5 %all-gather.16.cloned.1.call-start = ((), (), s32[]{:S(2)}) async-start(), calls=%async_computation.18 | async-start | bytes 4718592 | tf_op jit(solution)/shard_map/all_gather | solution.py:123
  169.5 38.6 %all-to-all-start.1 = ((bf16[8,8,128,128]{3,2,1,0:T(8,128)(2,1)}), bf16[8,8,128,128]{3,2,1,0:T(8,128)(2,1)}, u32[]{:S(2)}, u32[]{:S(2)}) async-start(bf16[8,8,128,128]{3,2,1,0:T(8,128)(2,1)} %stack.23), calls=%async_computation.2 | async-start | bytes 4194304 | tf_op jit(solution)/shard_map/all_to_all | solution.py:125
  173.9 235.2 %reduce-scatter.18.cloned.1.call-start = ((), (), s32[]{:S(2)}) async-start(), calls=%async_computation.21 | async-start | bytes 2621440 | tf_op jit(solution)/shard_map/reduce_scatter | solution.py:257
  344.7 92.1 %reduce-scatter.16.cloned.1.call-start = ((), (), s32[]{:S(2)}) async-start(), calls=%async_computation.19 | async-start | bytes 1310720 | tf_op jit(solution)/shard_map/reduce_scatter | solution.py:211
  409.1 56.7 %all-gather.20.cloned.1.call-start = ((), (), s32[]{:S(2)}) async-start(), calls=%async_computation.22 | async-start | bytes 1310720 | tf_op jit(solution)/shard_map/all_gather | solution.py:266
  439.2 64.3 %reduce-scatter.20.cloned.1.call-start = ((), (), s32[]{:S(2)}) async-start(), calls=%async_computation.23 | async-start | bytes 1310720 | tf_op jit(solution)/shard_map/reduce_scatter | solution.py:290
  476.6 79.6 %reduce-scatter.30.cloned.1.call-start = ((), (), s32[]{:S(2)}) async-start(), calls=%async_computation.28 | async-start | bytes 4718592 | tf_op jit(solution)/shard_map/reduce_scatter | solution.py:251
  483.2 127.6 %reduce-scatter.32.cloned.1.call-start = ((), (), s32[]{:S(2)}) async-start(), calls=%async_computation.29 | async-start | bytes 4718592 | tf_op jit(solution)/shard_map/reduce_scatter | solution.py:251
  490.7 159.7 %reduce-scatter.24.cloned.1.call-start = ((), (), s32[]{:S(2)}) async-start(), calls=%async_computation.25 | async-start | bytes 1179648 | tf_op jit(solution)/shard_map/reduce_scatter | solution.py:308
  493.3 194.1 %reduce-scatter.34.cloned.1.call-start = ((), (), s32[]{:S(2)}) async-start(), calls=%async_computation.30 | async-start | bytes 589824
  506.2 226.1 %reduce-scatter.22.cloned.1.call-start = ((), (), s32[]{:S(2)}) async-start(), calls=%async_computation.24 | async-start | bytes 2359296 | tf_op jit(solution)/shard_map/reduce_scatter | solution.py:307
  508.3 298.6 %reduce-scatter.26.cloned.1.call-start = ((), (), s32[]{:S(2)}) async-start(), calls=%async_computation.26 | async-start | bytes 9437184 | tf_op jit(solution)/shard_map/reduce_scatter | solution.py:250
  517.1 364.5 %reduce-scatter.28.cloned.1.call-start = ((), (), s32[]{:S(2)}) async-start(), calls=%async_computation.27 | async-start | bytes 9437184 | tf_op jit(solution)/shard_map/reduce_scatter | solution.py:250
  616.0 84.0 %copy-start.76 = (f32[2,128]{1,0:T(2,128)S(1)}, f32[2,128]{1,0:T(2,128)}, u32[]{:S(2)}) copy-start(f32[2,128]{1,0:T(2,128)} %param.23) | copy-start | bytes 3076
  616.0 116.3 %copy-start.28 = (f32[4,128,128]{1,2,0:T(8,128)S(1)}, f32[4,128,128]{1,2,0:T(8,128)}, u32[]{:S(2)}) copy-start(f32[4,128,128]{1,2,0:T(8,128)} %copy-done.27) | copy-start | bytes 786436
  700.0 108.2 %copy-start.75 = (f32[2,128]{1,0:T(2,128)}, f32[2,128]{1,0:T(2,128)S(1)}, u32[]{:S(2)}) copy-start(f32[2,128]{1,0:T(2,128)S(1)} %psum.7) | copy-start | bytes 3076
  (76 other events, 881.4 us)
Sparse Core Ops, SparseCore 0:
  21.9 28.2 all-gather.7
  52.7 22.8 all-gather.9
  86.0 43.6 reduce-scatter.13
  131.1 44.8 all-gather.17
  177.9 26.7 all-gather.11
  207.1 35.9 all-gather.13
  245.6 36.5 all-gather.15
  344.8 43.8 reduce-scatter.17
  409.2 27.5 reduce-scatter.15
  439.3 26.4 all-gather.19
  476.8 26.6 reduce-scatter.19
  506.7 49.5 reduce-scatter.29
  559.6 51.0 reduce-scatter.31
  614.4 35.9 reduce-scatter.23
  653.3 34.0 reduce-scatter.33
  691.2 41.0 reduce-scatter.21
  735.6 71.2 reduce-scatter.25
  810.2 71.2 reduce-scatter.27
